TPU v7x, 512 devices: a whole 4x4x16 slice. The times are simulated.
512 devices in a mesh: expert: 32 (over z, x_lo), fsdp: 16 (over x_hi, y, core).
Axes of the slice: x: 4 (x_hi: 2, x_lo: 2; x = x_hi * 2 + x_lo), y: 4, z: 16, core: 2. Of those that a mesh axis runs over, the one named last changes fastest.
Arguments:
- tokens: bfloat16 [3584, 4096], P(('expert', 'fsdp')), may hold values from -6 to 6
- expert_ids: int32 [3584, 8], P(('expert', 'fsdp')), may hold values from 0 to 31, all different within a row; in each aligned block of 7 rows (0 to 6, 7 to 13, ...) at most 2 rows name the same one
- gate_scores: float32 [3584, 8], P(('expert', 'fsdp')), may hold values from 0.05 to 1
- w_gate: bfloat16 [32, 1536, 4096], P('expert', 'fsdp'), may hold values from -0.09375 to 0.09375
- w_up: bfloat16 [32, 1536, 4096], P('expert', 'fsdp'), may hold values from -0.09375 to 0.09375
- w_down: bfloat16 [32, 1536, 4096], P('expert', None, 'fsdp'), may hold values from -0.15625 to 0.15625
Outputs:
- mixed: bfloat16 [3584, 4096], P(('expert', 'fsdp'))
Inputs may be any that keep to these rules, and one draw needn't show every extreme that they name: `expert_ids`: each token names 8 different experts. Within the 7 tokens of one device (aligned blocks of rows) no expert is named more than 2 times, and in every draw some expert is named exactly 2 times in some block.
All inputs are finite; a program needn't handle non-finite values.
Results may differ from a plain program's by a relative error of at most 0.0057.
Values may be sent and summed in bfloat16 or wider, within the bound.
A program may use at most 64 MiB of HBM per device.

v0:
```python
import jax
import jax.numpy as jnp
from jax import lax
from jax.sharding import PartitionSpec as P


def on_device(tokens, expert_ids, gate_scores, w_gate, w_up, w_down):
    n_expert = lax.axis_size("expert")
    n_fsdp = lax.axis_size("fsdp")
    local_tok, top_k = expert_ids.shape
    per_column = w_gate.shape[0]
    experts = per_column * n_expert
    capacity = min(local_tok, max(2, 3 * local_tok * top_k // (2 * experts)))
    width = tokens.shape[1]
    feature_cols = w_down.shape[2]
    weights = gate_scores / jnp.sum(gate_scores, axis=1, keepdims=True)
    expert_iota = lax.broadcasted_iota(jnp.int32, (1, 1, experts), 2)
    matches = (expert_ids[:, :, None] == expert_iota).astype(jnp.int32)
    chosen = jnp.sum(matches, axis=1, dtype=jnp.int32)
    weight_table = jnp.sum(weights[:, :, None] * matches.astype(jnp.float32), axis=1)
    ranks = jnp.cumsum(chosen, axis=0, dtype=jnp.int32) - chosen
    slot_iota = lax.broadcasted_iota(jnp.int32, (1, 1, capacity), 2)
    slot_mask = jnp.logical_and(ranks[:, :, None] == slot_iota, chosen[:, :, None] > 0)
    select_f32 = jnp.transpose(slot_mask.astype(jnp.float32), (1, 2, 0))
    select_bf = select_f32.astype(jnp.bfloat16)
    combine_table = select_f32 * jnp.transpose(weight_table)[:, None, :]
    outgoing = jnp.einsum("ect,td->ecd", select_bf, tokens, preferred_element_type=jnp.float32)
    outgoing = outgoing.astype(jnp.bfloat16)
    arrived = lax.all_to_all(outgoing, "expert", split_axis=0, concat_axis=0, tiled=True)
    portion = lax.all_gather(arrived[None], "fsdp", axis=0, tiled=True)
    routed = portion.reshape(portion.shape[0], n_expert, per_column, capacity, width)
    gate_act = jnp.einsum("knjcd,jhd->knjch", routed, w_gate, preferred_element_type=jnp.float32)
    up_act = jnp.einsum("knjcd,jhd->knjch", routed, w_up, preferred_element_type=jnp.float32)
    hidden = (jax.nn.silu(gate_act) * up_act).astype(jnp.bfloat16)
    summed = jnp.einsum(
        "fnjch,jhd->fnjcd",
        lax.all_gather(hidden, "fsdp", axis=4, tiled=True),
        w_down,
        preferred_element_type=jnp.float32,
    )
    expert_out = summed.astype(jnp.bfloat16).reshape(
        n_fsdp, n_expert, per_column * capacity, feature_cols
    )
    returned = lax.all_to_all(
        lax.all_to_all(expert_out, "expert", split_axis=1, concat_axis=1, tiled=True),
        "fsdp",
        split_axis=0,
        concat_axis=3,
        tiled=True,
    )
    returned = returned.reshape(experts, capacity, width)
    mixed = jnp.einsum(
        "ect,ecd->td", combine_table, returned.astype(jnp.float32), precision=lax.Precision.HIGHEST
    )
    return mixed.astype(jnp.bfloat16)


def solution(mesh):
    placed = (
        P(("expert", "fsdp"), None),
        P(("expert", "fsdp"), None),
        P(("expert", "fsdp"), None),
        P("expert", "fsdp", None),
        P("expert", "fsdp", None),
        P("expert", None, "fsdp"),
    )
    return jax.shard_map(
        on_device,
        mesh=mesh,
        in_specs=placed,
        out_specs=P(("expert", "fsdp"), None),
        check_vma=False,
    )
```

profile of v0, /device:TPU:1, one launch (start us, length us, event | category | flops | bytes accessed | tf_op | source)
XLA Modules:
  0.0 343.0 jit_solution(12220957122521888835)
XLA Ops:
  6.5 0.0 copy-start
  6.5 0.0 all-gather.6.cloned.1.call-start
  6.5 0.8 convert_reduce_fusion
  7.4 1.2 convolution_convert_fusion
  8.6 0.5 copy.34
  9.2 48.1 %all_to_all.25 = bf16[32,2,4096]{2,1,0:T(2,128)(2,1)S(1)} all-to-all(bf16[32,2,4096]{2,1,0:T(2,128)(2,1)S(1)} %copy.34), channel_id=1, replica_groups=mesh['expert'=32,'fsdp'=16] {'expert'}, dimensions={0} | all-to-all | bytes 1048576 | tf_op jit(solution)/shard_map/all_to_all | solution.py:29
  57.3 1.1 copy.35
  58.4 0.0 all-gather.6.cloned.1.call-update
  58.4 0.0 all-gather.4.cloned.1.call-start
  58.5 82.3 %all-gather.6.cloned.1.call-done = bf16[512,2,4096]{2,0,1:T(8,128)(2,1)} async-done(((bf16[32,2,4096]{2,0,1:T(8,128)(2,1)}), bf16[512,2,4096]{2,0,1:T(8,128)(2,1)}) %all-gather.6.cloned.1.call-update) | async-done | bytes 8388624 | tf_op jit(solution)/shard_map/all_gather | solution.py:30
  140.8 0.0 copy-start.3
  140.8 0.0 copy-start.4
  140.8 6.0 %fusion.10 = f32[16,32,1,2,96]{4,1,3,0,2:T(8,128)S(1)} fusion(bf16[16,32,2,4096]{3,1,0,2:T(8,128)(2,1)} %bitcast.65, bf16[1,96,4096]{2,1,0:T(8,128)(2,1)} %param.9), kind=kOutput, calls=%fused_computation.10 | convolution fusion | flops 805306368 | bytes 9568256 | tf_op jit(solution)/shard_map/knjcd,jhd->knjch/dot_general | solution.py:32
  146.8 0.0 copy-done.3
  146.8 0.1 copy-done.4
  146.9 2.3 fusion.19
  149.3 2.1 copy.38
  151.3 0.0 all-gather.4.cloned.1.call-update
  151.4 103.8 %all-gather.4.cloned.1.call-done = bf16[16,32,1,2,1536]{1,0,3,2,4:T(8,128)(2,1)} async-done(((bf16[16,32,1,2,96]{1,0,3,2,4:T(8,128)(2,1)}), bf16[16,32,1,2,1536]{1,0,3,2,4:T(8,128)(2,1)}) %all-gather.4.cloned.1.call-update) | async-done | bytes 3145744 | tf_op jit(solution)/shard_map/all_gather | solution.py:37
  255.2 13.4 %copy.39 = bf16[16,32,1,2,1536]{4,1,3,0,2:T(8,128)(2,1)} copy(bf16[16,32,1,2,1536]{1,0,3,2,4:T(8,128)(2,1)} %all-gather.4.cloned.1.call-done) | data formatting | bytes 6291456 | tf_op jit(solution)/shard_map/all_gather | solution.py:37
  268.6 0.0 copy-done
  268.6 0.0 copy-start.2
  268.6 0.0 copy-start.1
  268.6 2.9 fusion.7
  271.5 0.5 copy.40
  272.0 44.3 %all_to_all.26 = bf16[16,32,2,256]{3,2,0,1:T(2,128)(2,1)S(1)} all-to-all(bf16[16,32,2,256]{3,2,0,1:T(2,128)(2,1)S(1)} %copy.40), channel_id=1, replica_groups=mesh['expert'=32,'fsdp'=16] {'expert'}, dimensions={1} | all-to-all | bytes 1048576 | tf_op jit(solution)/shard_map/all_to_all | solution.py:45
  316.4 1.3 copy.41
  317.7 5.8 %all-to-all-start.2 = ((bf16[16,32,2,256]{3,2,1,0:T(2,128)(2,1)}), bf16[16,32,2,256]{3,2,1,0:T(2,128)(2,1)S(1)}, u32[]{:S(2)}, u32[]{:S(2)}) async-start(bf16[16,32,2,256]{3,2,1,0:T(2,128)(2,1)} %copy.41), calls=%async_computation.2 | async-start | bytes 1048576 | tf_op jit(solution)/shard_map/all_to_all | solution.py:44
  323.4 0.0 copy-done.2
  323.4 0.1 reduce_sum.28
  323.6 0.1 broadcast_divide_fusion
  323.6 0.0 copy-done.1
  323.6 0.1 fusion.27
  323.7 10.9 %all-to-all-done.2 = bf16[16,32,2,256]{3,2,1,0:T(2,128)(2,1)S(1)} async-done(((bf16[16,32,2,256]{3,2,1,0:T(2,128)(2,1)}), bf16[16,32,2,256]{3,2,1,0:T(2,128)(2,1)S(1)}, u32[]{:S(2)}, u32[]{:S(2)}) %all-to-all-start.2) | async-done | bytes 524320 | tf_op jit(solution)/shard_map/all_to_all | solution.py:44
  334.6 0.3 copy.42
  334.9 0.2 reshape.47
  335.2 1.0 fusion.4
  (3 shorter events, 0.0 us)
Async XLA Ops:
  6.5 262.1 %copy-start = (bf16[1,1536,256]{2,1,0:T(8,128)(2,1)S(1)}, bf16[1,1536,256]{2,1,0:T(8,128)(2,1)}, u32[]{:S(2)}) copy-start(bf16[1,1536,256]{2,1,0:T(8,128)(2,1)} %param.11) | copy-start | bytes 2359300
  6.5 134.3 %all-gather.6.cloned.1.call-start = ((), (), s32[]{:S(2)}) async-start(), calls=%async_computation.4 | async-start | bytes 8912896 | tf_op jit(solution)/shard_map/all_gather | solution.py:30
  58.4 196.7 %all-gather.4.cloned.1.call-start = ((), (), s32[]{:S(2)}) async-start(), calls=%async_computation.3 | async-start | bytes 13369344 | tf_op jit(solution)/shard_map/all_gather | solution.py:37
  140.8 6.0 %copy-start.3 = (bf16[512,2,4096]{2,0,1:T(8,128)(2,1)S(1)}, bf16[512,2,4096]{2,0,1:T(8,128)(2,1)}, u32[]{:S(2)}) copy-start(bf16[512,2,4096]{2,0,1:T(8,128)(2,1)} %all-gather.6.cloned.1.call-done) | copy-start | bytes 25165828
  140.8 6.1 %copy-start.4 = (bf16[1,96,4096]{2,1,0:T(8,128)(2,1)S(1)}, bf16[1,96,4096]{2,1,0:T(8,128)(2,1)}, u32[]{:S(2)}) copy-start(bf16[1,96,4096]{2,1,0:T(8,128)(2,1)} %param.10) | copy-start | bytes 2359300
  268.6 54.9 %copy-start.2 = (f32[7,8]{1,0:T(8,128)S(1)}, f32[7,8]{1,0:T(8,128)}, u32[]{:S(2)}) copy-start(f32[7,8]{1,0:T(8,128)} %param.8) | copy-start | bytes 676
  268.6 55.1 %copy-start.1 = (s32[7,8]{1,0:T(8,128)S(1)}, s32[7,8]{1,0:T(8,128)}, u32[]{:S(2)}) copy-start(s32[7,8]{1,0:T(8,128)} %param.7) | copy-start | bytes 676
  317.7 16.9 %all-to-all-start.2 = ((bf16[16,32,2,256]{3,2,1,0:T(2,128)(2,1)}), bf16[16,32,2,256]{3,2,1,0:T(2,128)(2,1)S(1)}, u32[]{:S(2)}, u32[]{:S(2)}) async-start(bf16[16,32,2,256]{3,2,1,0:T(2,128)(2,1)} %copy.41), calls=%async_computation.2 | async-start | bytes 1048576 | tf_op jit(solution)/shard_map/all_to_all | solution.py:44
Sparse Core Ops, SparseCore 0:
  58.6 82.1 all-gather.5
  151.5 103.6 all-gather.3
where the time goes:
time: 344 us; the launch traced here: 343 us
  waiting for transfers between devices  197 us (57%)
  blocking collectives  92.5 us (27%)
  local copies, waits for them, and re-layouts  19.6 us (6%)
  between operations  13.5 us (4%)
  matrix products  13.4 us (4%)
  starting transfers between devices  5.81 us (2%)
    all_gather x1, waiting for transfers between devices, on_device(): lax.all_gather(hidden, 'fsdp', axis=4, tiled=True)  104 us
    all_gather x1, waiting for transfers between devices, on_device(): portion = lax.all_gather(arrived[None], 'fsdp', axis=0, tiled=True)  82.3 us
    all_to_all x1, blocking collectives, on_device(): lax.all_to_all(outgoing, 'expert', split_axis=0, concat_axis=0, tiled=True)  48.1 us
    all_to_all x1, blocking collectives, on_device(): lax.all_to_all(expert_out, 'expert', split_axis=1, concat_axis=1, tiled=T...  44.3 us
    all_gather x1, local copies, waits for them, and re-layouts, on_device(): lax.all_gather(hidden, 'fsdp', axis=4, tiled=True)  13.4 us
    all_to_all x1, waiting for transfers between devices, on_device(): lax.all_to_all(lax.all_to_all(expert_out, 'expert', split_axis=1, concat_...  10.9 us
  transfers between devices with their start and end apart: 3, of which 3 were waited for; matrix products, arithmetic and copies ran while one was open for 0% of the time, Pallas kernels for 0%

commit v1 on v0

--- a/solution.py
+++ b/solution.py
@@ -41,12 +41,20 @@
     expert_out = summed.astype(jnp.bfloat16).reshape(
         n_fsdp, n_expert, per_column * capacity, feature_cols
     )
-    returned = lax.all_to_all(
-        lax.all_to_all(expert_out, "expert", split_axis=1, concat_axis=1, tiled=True),
-        "fsdp",
-        split_axis=0,
-        concat_axis=3,
-        tiled=True,
+    returned = jnp.concatenate(
+        lax.all_to_all(
+            jnp.stack(
+                jnp.split(
+                    lax.all_to_all(expert_out, "expert", split_axis=1, concat_axis=1, tiled=True),
+                    lax.axis_size("fsdp"),
+                    axis=0,
+                )
+            ),
+            "fsdp",
+            0,
+            0,
+        ),
+        axis=3,
     )
     returned = returned.reshape(experts, capacity, width)
     mixed = jnp.einsum(

time: 344 us -> 352 us (1.023)
  local copies, waits for them, and re-layouts: 19.6 us -> 28.4 us
    unnamed x10 -> x25, local copies, waits for them, and re-layouts: 0.13 us -> 9.57 us
where the time goes in v1:
time: 352 us
  waiting for transfers between devices  197 us (56%)
  blocking collectives  92.5 us (26%)
  local copies, waits for them, and re-layouts  28.4 us (8%)
  between operations  13.5 us (4%)
  matrix products  13.4 us (4%)
  starting transfers between devices  5.81 us (2%)
    all_gather x1, waiting for transfers between devices, on_device(): lax.all_gather(hidden, 'fsdp', axis=4, tiled=True)  104 us
    all_gather x1, waiting for transfers between devices, on_device(): portion = lax.all_gather(arrived[None], 'fsdp', axis=0, tiled=True)  82.3 us
    all_to_all x1, blocking collectives, on_device(): lax.all_to_all(outgoing, 'expert', split_axis=0, concat_axis=0, tiled=True)  48.1 us
    all_to_all x1, blocking collectives, on_device(): lax.all_to_all(expert_out, 'expert', split_axis=1, concat_axis=1, tiled=T...  44.3 us
    all_gather x1, local copies, waits for them, and re-layouts, on_device(): lax.all_gather(hidden, 'fsdp', axis=4, tiled=True)  13.4 us
    all_to_all x1, waiting for transfers between devices, on_device(): lax.all_to_all(jnp.stack(jnp.split(lax.all_to_all(expert_out, 'expert', s...  10.9 us
    unnamed x25, local copies, waits for them, and re-layouts  9.57 us
  transfers between devices with their start and end apart: 3, of which 3 were waited for; matrix products, arithmetic and copies ran while one was open for 0% of the time, Pallas kernels for 0%

profile of v1, /device:TPU:1, one launch (start us, length us, event | category | flops | bytes accessed | tf_op | source)
XLA Modules:
  0.0 351.8 jit_solution(1371453279640389816)
XLA Ops:
  6.5 0.0 copy-start
  6.5 0.0 all-gather.6.cloned.1.call-start
  6.5 0.8 convert_reduce_fusion
  7.4 1.2 convolution_convert_fusion
  8.6 0.5 copy.55
  9.2 48.1 %all_to_all.15 = bf16[32,2,4096]{2,1,0:T(2,128)(2,1)S(1)} all-to-all(bf16[32,2,4096]{2,1,0:T(2,128)(2,1)S(1)} %copy.55), channel_id=1, replica_groups=mesh['expert'=32,'fsdp'=16] {'expert'}, dimensions={0} | all-to-all | bytes 1048576 | tf_op jit(solution)/shard_map/all_to_all | solution.py:29
  57.3 1.1 copy.56
  58.4 0.0 all-gather.6.cloned.1.call-update
  58.4 0.0 all-gather.4.cloned.1.call-start
  58.5 82.3 %all-gather.6.cloned.1.call-done = bf16[512,2,4096]{2,0,1:T(8,128)(2,1)} async-done(((bf16[32,2,4096]{2,0,1:T(8,128)(2,1)}), bf16[512,2,4096]{2,0,1:T(8,128)(2,1)}) %all-gather.6.cloned.1.call-update) | async-done | bytes 8388624 | tf_op jit(solution)/shard_map/all_gather | solution.py:30
  140.8 6.0 %fusion.10 = f32[16,32,1,2,96]{4,1,3,0,2:T(8,128)S(1)} fusion(bf16[16,32,2,4096]{3,1,0,2:T(8,128)(2,1)} %bitcast.157, bf16[1,96,4096]{2,1,0:T(8,128)(2,1)} %param.9), kind=kOutput, calls=%fused_computation.10 | convolution fusion | flops 805306368 | bytes 9568256 | tf_op jit(solution)/shard_map/knjcd,jhd->knjch/dot_general | solution.py:32
  146.8 0.0 copy-done.3
  146.8 0.1 copy-done.4
  146.9 2.3 fusion.19
  149.3 2.1 copy.59
  151.3 0.0 all-gather.4.cloned.1.call-update
  151.4 103.8 %all-gather.4.cloned.1.call-done = bf16[16,32,1,2,1536]{1,0,3,2,4:T(8,128)(2,1)} async-done(((bf16[16,32,1,2,96]{1,0,3,2,4:T(8,128)(2,1)}), bf16[16,32,1,2,1536]{1,0,3,2,4:T(8,128)(2,1)}) %all-gather.4.cloned.1.call-update) | async-done | bytes 3145744 | tf_op jit(solution)/shard_map/all_gather | solution.py:37
  255.2 13.4 %copy.60 = bf16[16,32,1,2,1536]{4,1,3,0,2:T(8,128)(2,1)} copy(bf16[16,32,1,2,1536]{1,0,3,2,4:T(8,128)(2,1)} %all-gather.4.cloned.1.call-done) | data formatting | bytes 6291456 | tf_op jit(solution)/shard_map/all_gather | solution.py:37
  268.6 0.0 copy-done
  268.6 2.9 fusion.7
  271.5 0.5 copy.61
  272.0 44.3 %all_to_all.16 = bf16[16,32,2,256]{3,2,0,1:T(2,128)(2,1)S(1)} all-to-all(bf16[16,32,2,256]{3,2,0,1:T(2,128)(2,1)S(1)} %copy.61), channel_id=1, replica_groups=mesh['expert'=32,'fsdp'=16] {'expert'}, dimensions={1} | all-to-all | bytes 1048576 | tf_op jit(solution)/shard_map/all_to_all | solution.py:48
  316.4 0.6 constant_dynamic-update-slice_fusion.15
  317.0 0.6 constant_dynamic-update-slice_fusion.14
  317.6 0.6 constant_dynamic-update-slice_fusion.13
  318.3 0.6 constant_dynamic-update-slice_fusion.12
  318.9 0.6 constant_dynamic-update-slice_fusion.11
  319.5 0.6 constant_dynamic-update-slice_fusion.10
  320.2 0.6 constant_dynamic-update-slice_fusion.9
  320.8 0.6 constant_dynamic-update-slice_fusion.8
  321.4 0.6 constant_dynamic-update-slice_fusion.7
  322.1 0.6 constant_dynamic-update-slice_fusion.6
  322.7 0.6 constant_dynamic-update-slice_fusion.5
  323.3 0.6 constant_dynamic-update-slice_fusion.4
  324.0 0.6 constant_dynamic-update-slice_fusion.3
  324.6 0.6 constant_dynamic-update-slice_fusion.2
  325.2 0.6 constant_dynamic-update-slice_fusion.1
  325.8 0.6 constant_dynamic-update-slice_fusion
  326.5 5.8 %all-to-all-start.2 = ((bf16[16,1,32,2,256]{4,3,2,1,0:T(2,128)(2,1)}), bf16[16,1,32,2,256]{4,3,2,1,0:T(2,128)(2,1)S(1)}, u32[]{:S(2)}, u32[]{:S(2)}) async-start(bf16[16,1,32,2,256]{4,3,2,1,0:T(2,128)(2,1)} %constant_dynamic-update-slice_fusion), calls=%async_computation.2 | async-start | bytes 1048576 | tf_op jit(solution)/shard_map/all_to_all | solution.py:45
  332.2 0.0 copy-done.2
  332.2 0.1 reduce_sum.28
  332.4 0.1 broadcast_divide_fusion
  332.4 0.0 copy-done.1
  332.4 0.1 fusion.27
  332.5 10.9 %all-to-all-done.2 = bf16[16,1,32,2,256]{4,3,2,1,0:T(2,128)(2,1)S(1)} async-done(((bf16[16,1,32,2,256]{4,3,2,1,0:T(2,128)(2,1)}), bf16[16,1,32,2,256]{4,3,2,1,0:T(2,128)(2,1)S(1)}, u32[]{:S(2)}, u32[]{:S(2)}) %all-to-all-start.2) | async-done | bytes 524320 | tf_op jit(solution)/shard_map/all_to_all | solution.py:45
  343.4 0.3 copy.77
  343.7 0.2 reshape_reshape.3
  343.9 1.0 fusion.4
  (7 shorter events, 0.0 us)
Async XLA Ops:
  6.5 262.1 %copy-start = (bf16[1,1536,256]{2,1,0:T(8,128)(2,1)S(1)}, bf16[1,1536,256]{2,1,0:T(8,128)(2,1)}, u32[]{:S(2)}) copy-start(bf16[1,1536,256]{2,1,0:T(8,128)(2,1)} %param.11) | copy-start | bytes 2359300
  6.5 134.3 %all-gather.6.cloned.1.call-start = ((), (), s32[]{:S(2)}) async-start(), calls=%async_computation.4 | async-start | bytes 8912896 | tf_op jit(solution)/shard_map/all_gather | solution.py:30
  58.4 196.7 %all-gather.4.cloned.1.call-start = ((), (), s32[]{:S(2)}) async-start(), calls=%async_computation.3 | async-start | bytes 13369344 | tf_op jit(solution)/shard_map/all_gather | solution.py:37
  140.8 6.0 %copy-start.3 = (bf16[512,2,4096]{2,0,1:T(8,128)(2,1)S(1)}, bf16[512,2,4096]{2,0,1:T(8,128)(2,1)}, u32[]{:S(2)}) copy-start(bf16[512,2,4096]{2,0,1:T(8,128)(2,1)} %all-gather.6.cloned.1.call-done) | copy-start | bytes 25165828
  140.8 6.1 %copy-start.4 = (bf16[1,96,4096]{2,1,0:T(8,128)(2,1)S(1)}, bf16[1,96,4096]{2,1,0:T(8,128)(2,1)}, u32[]{:S(2)}) copy-start(bf16[1,96,4096]{2,1,0:T(8,128)(2,1)} %param.10) | copy-start | bytes 2359300
  268.6 63.7 %copy-start.2 = (f32[7,8]{1,0:T(8,128)S(1)}, f32[7,8]{1,0:T(8,128)}, u32[]{:S(2)}) copy-start(f32[7,8]{1,0:T(8,128)} %param.8) | copy-start | bytes 676
  268.6 63.9 %copy-start.1 = (s32[7,8]{1,0:T(8,128)S(1)}, s32[7,8]{1,0:T(8,128)}, u32[]{:S(2)}) copy-start(s32[7,8]{1,0:T(8,128)} %param.7) | copy-start | bytes 676
  326.5 16.9 %all-to-all-start.2 = ((bf16[16,1,32,2,256]{4,3,2,1,0:T(2,128)(2,1)}), bf16[16,1,32,2,256]{4,3,2,1,0:T(2,128)(2,1)S(1)}, u32[]{:S(2)}, u32[]{:S(2)}) async-start(bf16[16,1,32,2,256]{4,3,2,1,0:T(2,128)(2,1)} %constant_dynamic-update-slice_fusion), calls=%async_computation.2 | async-start | bytes 1048576 | tf_op jit(solution)/shard_map/all_to_all | solution.py:45
Sparse Core Ops, SparseCore 0:
  58.6 82.1 all-gather.5
  151.5 103.6 all-gather.3
